TPU v7x, 1024 devices: a whole 4x8x16 slice. The times are simulated.
1024 devices in a mesh: ctx: 16 (over y, core), chan: 64 (over x, z).
Axes of the slice: x: 4, y: 8, z: 16, core: 2. Of those that a mesh axis runs over, the one named last changes fastest.
Arguments:
- features: float32 [3, 2048, 8192], P(None, 'ctx', 'chan'), may hold values from -6 to 6
- saved_conv: float32 [2048, 8192], P('ctx', 'chan'), may hold values from -6 to 6
- out_grad: float32 [2048, 8192], P('ctx', 'chan'), may hold values from -16 to 16
- short_filter: float32 [3, 3, 8192], P(None, None, 'chan'), may hold values from -3 to 3
- residue: float32 [8192, 16], P('chan'), may hold values from -0.18 to 0.18
- rate: float32 [8192, 16], P('chan'), may hold values from 4.8828125e-05 to 0.0333333333
- bias: float32 [8192], P('chan'), may hold values from -1 to 1
- w_proj: bfloat16 [3, 8192, 8192], P(None, 'chan'), may hold values from -0.0625 to 0.0625
Outputs:
- grad_inputs: float32 [3, 2048, 8192], P(None, 'ctx', 'chan')
- grad_x: float32 [2048, 8192], P('ctx', 'chan')
- grad_residue: float32 [8192, 16], P('chan')
- grad_bias: float32 [8192], P('chan')
All inputs are finite; a program needn't handle non-finite values.
Results may differ from a plain program's by a relative error of at most 0.0029.
Values may be sent and summed in bfloat16 or wider, within the bound.
A program may use at most 64 MiB of HBM per device.

v0:
```python
import jax
import jax.numpy as jnp
from jax import lax
from jax.sharding import PartitionSpec as P

STRETCH = 64


def carried_in(part, axis, combine, identity):
    count = lax.axis_size(axis)
    place = lax.axis_index(axis)
    ahead = count - 1 - place
    gathered = jax.tree.map(lambda a: lax.all_gather(a, axis), part)
    state = jax.tree.map(lambda a, e: jnp.zeros_like(a) + jnp.asarray(e, a.dtype), part, identity)

    def one(hop, state):
        source = count - 1 - hop
        return combine(
            state, jax.tree.map(lambda a: lax.dynamic_index_in_dim(a, source, 0, False), gathered)
        )

    return lax.fori_loop(0, ahead, one, state)


def from_behind(array, axis, by):
    count = lax.axis_size(axis)
    pairs = [(i, i + by) for i in range(count) if 0 <= i + by < count]
    return lax.ppermute(array, axis, pairs)


def body(features, saved_conv, out_grad, short_filter, residue, rate, bias, w_proj):
    highest = lax.Precision.HIGHEST
    gate_feat = features[0]
    key_feat = features[1]
    value_feat = features[2]
    tok_rows, channels = out_grad.shape
    blocks = tok_rows // STRETCH
    product = key_feat * value_feat
    signal = out_grad * gate_feat
    grad_gate = out_grad * (saved_conv + bias * product)
    offsets = jnp.arange(STRETCH, dtype=jnp.float32)
    powers = jnp.exp(-rate[None] * offsets[:, None, None])
    remaining = jnp.exp(-rate[None] * (STRETCH - offsets)[:, None, None])
    sig_blocks = signal.reshape(blocks, STRETCH, channels)
    prod_blocks = product.reshape(blocks, STRETCH, channels)
    summaries = jnp.einsum("kjc,jcm->kcm", sig_blocks, powers, precision=highest)
    block_index = jnp.arange(blocks, dtype=jnp.float32)
    block_decay = jnp.exp(-rate[None] * (STRETCH * block_index)[:, None, None])
    own_total = jnp.sum(summaries * block_decay, axis=0)
    span_decay = jnp.exp(-rate * tok_rows)

    def combine(earlier, later_part):
        return (later_part[0] + later_part[1] * earlier[0], later_part[1] * earlier[1])

    identity = (jnp.zeros_like(own_total), jnp.ones_like(span_decay))
    incoming, span_unused = carried_in((own_total, span_decay), "ctx", combine, identity)
    stretch_decay = jnp.exp(-rate * STRETCH)

    def back_step(state, summary):
        return (summary + stretch_decay * state, state)

    first_state, block_ends = lax.scan(back_step, incoming, summaries, reverse=True)
    far_corr = jnp.einsum("jcm,kcm->kjc", residue[None] * remaining, block_ends, precision=highest)
    far_residue = jnp.einsum(
        "kjc,jcm,kcm->cm", prod_blocks, remaining, block_ends, precision=highest
    )
    taps = jnp.einsum("lcm,cm->lc", powers, residue, precision=highest)
    padded = jnp.pad(sig_blocks, ((0, 0), (0, STRETCH), (0, 0)))

    def shift_block(offset):
        return lax.dynamic_slice_in_dim(padded, offset, STRETCH, 1)

    shifted = jax.vmap(shift_block)(jnp.arange(STRETCH, dtype=jnp.int32))
    near_corr = jnp.einsum("lkjc,lc->kjc", shifted, taps, precision=highest)
    lagged = jnp.einsum("lkjc,kjc->lc", shifted, prod_blocks, precision=highest)
    near_residue = jnp.einsum("lc,lcm->cm", lagged, powers, precision=highest)
    corr = (near_corr + far_corr).reshape(tok_rows, channels)
    grad_prod = corr + bias * signal
    grad_stream = jnp.stack([grad_gate, grad_prod * value_feat, grad_prod * key_feat])
    next_rim = from_behind(grad_stream[:, 0:2], "ctx", -1)
    extended = jnp.concatenate([grad_stream, next_rim], axis=1)
    grad_inputs = short_filter[:, 0][:, None, :] * extended[:, 0:tok_rows]
    grad_inputs = grad_inputs + short_filter[:, 1][:, None, :] * extended[:, 1 : tok_rows + 1]
    grad_inputs = grad_inputs + short_filter[:, 2][:, None, :] * extended[:, 2 : tok_rows + 2]
    scale = (tok_rows * lax.axis_size("ctx")) ** (-0.5)
    summed_residue, summed_bias = lax.psum(
        (near_residue + far_residue, jnp.sum(signal * product, axis=0)), "ctx"
    )
    grad_residue = summed_residue * scale
    grad_bias = summed_bias * scale
    rounded = grad_inputs.astype(jnp.bfloat16)
    gathered_rows = lax.all_gather(rounded, "chan", axis=2, tiled=True)
    grad_x = jnp.einsum("ptc,pdc->td", gathered_rows, w_proj, preferred_element_type=jnp.float32)
    return (grad_inputs, grad_x, grad_residue, grad_bias)


def solution(mesh):
    return jax.shard_map(
        body,
        mesh=mesh,
        in_specs=(
            P(None, "ctx", "chan"),
            P("ctx", "chan"),
            P("ctx", "chan"),
            P(None, None, "chan"),
            P("chan", None),
            P("chan", None),
            P("chan"),
            P(None, "chan", None),
        ),
        out_specs=(P(None, "ctx", "chan"), P("ctx", "chan"), P("chan", None), P("chan")),
        check_vma=False,
    )
```

profile of v0, /device:TPU:16, one launch (start us, length us, event | category | flops | bytes accessed | tf_op | source)
XLA Modules:
  0.0 265.1 jit_solution(3964849686293031684)
XLA Ops:
  7.2 0.0 all-gather.4.cloned.1.call-start
  7.2 1.0 multiply_reduce_fusion.2
  8.2 0.1 copy.32
  8.3 0.1 copy.33
  8.4 0.8 copy.39
  9.2 0.8 copy.43
  10.0 0.7 multiply_exponential_fusion.7
  10.7 0.1 copy.31
  10.9 7.8 %gather_fusion = f32[64,2,64,128]{3,1,2,0:T(2,128)} fusion(f32[2,128,128]{2,0,1:T(2,128)S(1)} %pad.4, s32[64]{0:T(128)S(1)} %shift-left_bitcast_fusion), kind=kCustom, calls=%fused_computation | custom fusion | bytes 8389376 | tf_op jit(solution)/shard_map/vmap()/gather | solution.py:71
  18.6 8.7 %copy.46 = f32[64,2,64,128]{2,0,1,3:T(8,128)} copy(f32[64,2,64,128]{3,1,2,0:T(2,128)} %gather_fusion) | data formatting | bytes 8388608 | tf_op jit(solution)/shard_map/vmap()/gather | solution.py:71
  27.3 1.2 convolution_bitcast_fusion.2
  28.5 1.9 multiply_reduce_fusion.1
  30.5 28.2 %all-gather = f32[2048,16]{1,0:T(8,128)S(1)} all-gather(f32[128,16]{1,0:T(8,128)S(1)} %get-tuple-element.258), channel_id=2, replica_groups=mesh['ctx'=16,'chan'=64] {'ctx'}, dimensions={0}, use_global_device_ids=true | all-gather | bytes 139264 | tf_op jit(solution)/shard_map/all_gather | solution.py:13
  58.7 0.3 copy.36
  59.0 0.0 copy-start
  59.0 0.0 copy-start.2
  59.0 15.8 %all-gather.1 = f32[2048,16]{0,1:T(8,128)S(1)} all-gather(f32[128,16]{0,1:T(8,128)S(1)} %get-tuple-element.253), channel_id=3, replica_groups=mesh['ctx'=16,'chan'=64] {'ctx'}, dimensions={0}, use_global_device_ids=true | all-gather | bytes 139264 | tf_op jit(solution)/shard_map/all_gather | solution.py:13
  74.9 0.0 copy-start.1
  74.9 0.7 while.30
  75.6 0.1 copy.38
  75.6 0.1 while.31
  75.7 0.1 copy.40
  75.8 6.4 %fusion.19 = f32[128,1,2,64]{3,1,2,0:T(1,128)S(1)} fusion(f32[64,128,1,1]{0,2,3,1:T(1,128)S(1)} %convolution_bitcast_fusion.2, f32[64,2,64,128]{2,0,1,3:T(8,128)} %copy.46), kind=kOutput, calls=%fused_computation.55 | convolution fusion | flops 12582912 | bytes 4292608 | tf_op jit(solution)/shard_map/lkjc,lc->kjc/dot_general | solution.py:74
  82.3 1.4 fusion
  83.7 0.1 copy.41
  83.8 0.0 copy-done
  83.8 0.0 copy-done.2
  83.8 4.1 %collective-permute-start = (f32[3,2,128]{2,1,0:T(2,128)S(1)}, f32[3,2,128]{2,1,0:T(2,128)S(1)}, u32[]{:S(2)}, u32[]{:S(2)}) collective-permute-start(f32[3,2,128]{2,1,0:T(2,128)S(1)} %slice.39), channel_id=1, source_target_pairs={{64,0},{128,64},{192,128},{256,192},{320,256},{384,320},{448,384},... | collective-permute-start | bytes 9224 | tf_op jit(solution)/shard_map/ppermute | solution.py:28
  87.9 0.0 copy-done.1
  87.9 1.1 collective-permute-done
  89.0 0.8 fusion.16
  89.8 0.0 all-gather.4.cloned.1.call-update
  89.8 0.1 copy.61
  90.0 0.1 copy.42
  90.1 1.9 fusion.1
  92.0 0.1 copy.62
  92.1 0.1 copy.69
  92.2 4.5 %multiply_reduce_fusion = f32[128,64]{0,1:T(8,128)S(1)} fusion(f32[64,2,64,128]{3,1,2,0:T(2,128)} %gather_fusion, f32[128,64,2]{0,2,1:T(2,128)S(1)} %copy.69), kind=kLoop, calls=%fused_computation.5 | loop fusion | flops 2088960 | bytes 4292608
  96.6 0.1 copy.54
  96.7 1.9 fusion.3
  98.6 0.1 copy.56
  98.6 22.2 %all-reduce.1 = (f32[128,16]{0,1:T(8,128)S(1)}, f32[128]{0:T(128)S(1)}) all-reduce(f32[128,16]{0,1:T(8,128)S(1)} %bitcast_add_fusion.3, f32[128]{0:T(128)S(1)} %get-tuple-element.245), channel_id=1, replica_groups=mesh['ctx'=16,'chan'=64] {'ctx'}, use_global_device_ids=true, to_apply=%region_5.6 | all-reduce | flops 2176 | bytes 17408 | tf_op jit(solution)/shard_map/psum | solution.py:86
  120.8 0.5 broadcast_multiply_fusion.1
  121.4 0.6 broadcast_multiply_fusion
  122.0 129.3 %all-gather.4.cloned.1.call-done = bf16[3,128,8192]{2,1,0:T(8,128)(2,1)} async-done(((bf16[3,128,128]{2,1,0:T(8,128)(2,1)}), bf16[3,128,8192]{2,1,0:T(8,128)(2,1)}) %all-gather.4.cloned.1.call-update) | async-done | bytes 6291472 | tf_op jit(solution)/shard_map/all_gather | solution.py:92
  251.2 7.0 %convolution_bitcast_fusion.1 = f32[128,128]{1,0:T(8,128)} fusion(bf16[3,128,8192]{2,1,0:T(8,128)(2,1)} %all-gather.4.cloned.1.call-done, bf16[3,128,8192]{2,1,0:T(8,128)(2,1)} %param.19), kind=kOutput, calls=%fused_computation.11 | convolution fusion | flops 805306368 | bytes 12648448 | tf_op jit(solution)/shard_map/ptc,pdc->td/dot_general | solution.py:93
  (42 shorter events, 0.5 us)
Async XLA Ops:
  7.2 244.1 %all-gather.4.cloned.1.call-start = ((), (), s32[]{:S(2)}) async-start(), calls=%async_computation | async-start | bytes 6389760 | tf_op jit(solution)/shard_map/all_gather | solution.py:92
  59.0 24.7 %copy-start = (f32[3,128,128]{2,1,0:T(8,128)S(1)}, f32[3,128,128]{2,1,0:T(8,128)}, u32[]{:S(2)}) copy-start(f32[3,128,128]{2,1,0:T(8,128)} %param.12) | copy-start | bytes 589828
  59.0 24.8 %copy-start.2 = (f32[128]{0:T(128)S(1)}, f32[128]{0:T(128)}, u32[]{:S(2)}) copy-start(f32[128]{0:T(128)} %param.18) | copy-start | bytes 1540
  74.9 13.0 %copy-start.1 = (f32[3,3,128]{2,1,0:T(4,128)S(1)}, f32[3,3,128]{2,1,0:T(4,128)}, u32[]{:S(2)}) copy-start(f32[3,3,128]{2,1,0:T(4,128)} %param.15) | copy-start | bytes 13828
  83.8 5.2 %collective-permute-start = (f32[3,2,128]{2,1,0:T(2,128)S(1)}, f32[3,2,128]{2,1,0:T(2,128)S(1)}, u32[]{:S(2)}, u32[]{:S(2)}) collective-permute-start(f32[3,2,128]{2,1,0:T(2,128)S(1)} %slice.39), channel_id=1, source_target_pairs={{64,0},{128,64},{192,128},{256,192},{320,256},{384,320},{448,384},... | collective-permute-start | bytes 9224 | tf_op jit(solution)/shard_map/ppermute | solution.py:28
Sparse Core Ops, SparseCore 0:
  90.0 161.2 all-gather.3
where the time goes:
time: 266 us; the launch traced here: 265 us
  waiting for transfers between devices  130 us (49%)
  blocking collectives  66.2 us (25%)
  matrix products  21.8 us (8%)
  local copies, waits for them, and re-layouts  19.6 us (7%)
  between operations  14.3 us (5%)
  other arithmetic  8.32 us (3%)
  starting transfers between devices  4.09 us (2%)
    all_gather x1, waiting for transfers between devices, body(): gathered_rows = lax.all_gather(rounded, 'chan', axis=2, tiled=True)  129 us
    all_gather x2, blocking collectives, carried_in(): gathered = jax.tree.map(lambda a: lax.all_gather(a, axis), part)  44 us
    psum x1, blocking collectives, body(): lax.psum((near_residue + far_residue, jnp.sum(signal * product, axis=0)),...  22.2 us
    gather x2, local copies, waits for them, and re-layouts, shift_block(): return lax.dynamic_slice_in_dim(padded, offset, STRETCH, 1)  16.5 us
    dot_general x1, matrix products, body(): jnp.einsum('ptc,pdc->td', gathered_rows, w_proj, preferred_element_type=j...  7.02 us
    dot_general x1, matrix products, body(): near_corr = jnp.einsum('lkjc,lc->kjc', shifted, taps, precision=highest)  6.43 us
  transfers between devices with their start and end apart: 2, of which 2 were waited for; matrix products, arithmetic and copies ran while one was open for 4% of the time, Pallas kernels for 0%

commit v1 on v0

v1 whole, which is shorter than its diff:
```python
import jax
import jax.numpy as jnp
from jax import lax
from jax.experimental import pallas as pl
from jax.experimental.pallas import tpu as pltpu
from jax.sharding import PartitionSpec as P

NX = 4
MODES = 16
TOK = 128
LANES = 128
SHARES = 4
F32 = jnp.float32
BF16 = jnp.bfloat16
MESH = pl.DeviceIdType.MESH


def make_kernel(nctx, nz):
    ny = nctx // 2
    half = nz // 2
    width = nz * LANES
    share_rows = LANES // SHARES
    half_rows = share_rows // 2
    scale = (TOK * nctx) ** -0.5
    blocks = TOK // 8

    def kernel(feat, sconv, ograd, sfilt, residue, rate, bias, w,
               gi_out, gx_out, gr_out, gb_out,
               feat_v, sc_v, og_v, sf_v, res_v, rate_v, bias_v, sig_v, prod_v, corr_v, gs_v,
               base_v, d8_v, z_v, fsend, frecv, halo, gsend, grecv, abuf, wbuf, relay,
               acc_v, csend, crecv,
               in_sem, w_sem, f_ssem, f_rsem, h_ssem, h_rsem, g_ssem, g_rsem,
               a_ssem, a_rsem, b_ssem, b_rsem, c_ssem, c_rsem):
        ctx = lax.axis_index("ctx")
        chan = lax.axis_index("chan")
        x = chan // nz
        z = lax.rem(chan, nz)
        y = ctx // 2
        core = lax.rem(ctx, 2)

        def at_x(dx):
            return {"chan": lax.rem(x + dx + NX, NX) * nz + z}

        def at_z(dz):
            return {"chan": x * nz + lax.rem(z + dz + nz, nz)}

        def at_ctx(c):
            return {"ctx": c}

        def at_y(dy):
            return {"ctx": lax.rem(y + dy + ny, ny) * 2 + core}

        other = at_ctx(y * 2 + 1 - core)
        sign = 1 - 2 * core

        def remote(src, dst, ssem, rsem, device):
            return pltpu.make_async_remote_copy(
                src_ref=src, dst_ref=dst, send_sem=ssem, recv_sem=rsem,
                device_id=device, device_id_type=MESH)

        barrier = pltpu.get_barrier_semaphore()

        def greet(d, carry):
            pl.semaphore_signal(barrier, inc=1, device_id=at_ctx(lax.rem(ctx + d, nctx)),
                                device_id_type=MESH)
            return carry

        lax.fori_loop(1, nctx, greet, 0)
        for dx in range(1, NX):
            pl.semaphore_signal(barrier, inc=1, device_id=at_x(dx), device_id_type=MESH)
        for dz in (1, -1):
            pl.semaphore_signal(barrier, inc=1, device_id=at_z(dz), device_id_type=MESH)

        loads = [pltpu.make_async_copy(s, d, in_sem.at[i]) for i, (s, d) in enumerate((
            (feat, feat_v), (ograd, og_v), (rate, rate_v), (residue, res_v), (sconv, sc_v),
            (sfilt, sf_v), (bias, bias_v)))]
        for c in loads:
            c.start()
        own_rows = pl.ds(pl.multiple_of(x * LANES, LANES), LANES)
        own_w = pltpu.make_async_copy(
            w.at[:, :, pl.ds(pl.multiple_of(x * width, LANES), width)],
            wbuf.at[:, own_rows, :], w_sem.at[0])
        own_w.start()
        for c in loads:
            c.wait()

        sig_v[...] = og_v[...] * feat_v[0]
        prod_v[...] = feat_v[1] * feat_v[2]

        iota8 = lax.broadcasted_iota(jnp.int32, (8, LANES), 0).astype(F32)
        for m in range(MODES):
            rm = jnp.broadcast_to(rate_v[m:m + 1, :], (8, LANES))
            d8 = jnp.exp(rm * -8.0)
            up = jnp.exp(-rm * iota8)
            base_v[m] = jnp.exp(-rm * (8.0 - iota8))
            d8_v[m] = d8
            total = jnp.zeros((8, LANES), F32)
            for k in range(blocks):
                total = total + up * sig_v[8 * k:8 * k + 8, :]
                up = up * d8
            fsend[m:m + 1, :] = jnp.sum(total, axis=0, keepdims=True)

        pl.semaphore_wait(barrier, nctx - 1 + NX - 1 + 2)

        prev = at_ctx(lax.rem(ctx + nctx - 1, nctx))
        halo_copies = [
            remote(feat.at[:, 0:8, :], halo.at[0:3], h_ssem.at[0], h_rsem.at[0], prev),
            remote(ograd.at[0:8, :], halo.at[3], h_ssem.at[1], h_rsem.at[1], prev),
            remote(sconv.at[0:8, :], halo.at[4], h_ssem.at[2], h_rsem.at[2], prev)]
        for c in halo_copies:
            c.start()

        def f_copy(src_ctx, dst):
            return remote(fsend, frecv.at[src_ctx], f_ssem.at[dst], f_rsem.at[src_ctx], at_ctx(dst))

        def send_f(i, carry):
            f_copy(ctx, i).start()
            return carry

        lax.fori_loop(0, ctx, send_f, 0)

        share = 2 * lax.rem(y, 2) + core
        r0 = share * share_rows

        def rows_of(dx, first, count):
            return pl.ds(pl.multiple_of(lax.rem(x + dx + NX, NX) * LANES + first, 8), count)

        def cols_of(dx):
            return pl.ds(pl.multiple_of(lax.rem(x + dx + NX, NX) * width, LANES), width)

        mine = pl.ds(pl.multiple_of(r0, 8), share_rows)
        mine0 = pl.ds(pl.multiple_of(r0, 8), half_rows)
        mine1 = pl.ds(pl.multiple_of(r0 + half_rows, 8), half_rows)
        here = wbuf.at[:, rows_of(0, r0, share_rows), :]
        b_out0 = remote(w.at[:, mine0, cols_of(2)], relay.at[0], b_ssem.at[2], b_rsem.at[2], at_x(1))
        b_out1 = remote(w.at[:, mine1, cols_of(2)], relay.at[1], b_ssem.at[3], b_rsem.at[3], at_x(-1))
        b_right = remote(w.at[:, mine, cols_of(1)], here, b_ssem.at[0], b_rsem.at[0], at_x(1))
        b_left = remote(w.at[:, mine, cols_of(-1)], here, b_ssem.at[1], b_rsem.at[1], at_x(-1))
        for c in (b_out0, b_out1, b_right, b_left):
            c.start()
        b_relay0 = remote(relay.at[0], wbuf.at[:, rows_of(-1, r0, half_rows), :],
                          b_ssem.at[4], b_rsem.at[4], at_x(1))
        b_relay1 = remote(relay.at[1], wbuf.at[:, rows_of(1, r0 + half_rows, half_rows), :],
                          b_ssem.at[5], b_rsem.at[5], at_x(-1))

        def same_place(dx, first, count, sem, device):
            ref = wbuf.at[:, rows_of(dx, first, count), :]
            return remote(ref, ref, b_ssem.at[sem], b_rsem.at[sem], device)

        dec = jnp.exp(-rate_v[...])
        res = res_v[...]

        def scan_block(i, carry):
            state, total = carry
            first = pl.multiple_of(TOK - 8 - 8 * i, 8)
            sig8 = sig_v[pl.ds(first, 8), :]
            prod8 = prod_v[pl.ds(first, 8), :]
            rows = [None] * 8
            for t in range(7, -1, -1):
                state = sig8[t:t + 1, :] + dec * state
                total = total + prod8[t:t + 1, :] * state
                rows[t] = jnp.sum(res * state, axis=0, keepdims=True)
            corr_v[pl.ds(first, 8), :] = jnp.concatenate(rows, axis=0)
            return state, total

        zero = jnp.zeros((MODES, LANES), F32)
        _, near_grad = lax.fori_loop(0, blocks, scan_block, (zero, zero))

        for m in range(MODES):
            down = base_v[m]
            d8 = d8_v[m]
            total = jnp.zeros((8, LANES), F32)
            for k in range(blocks - 1, -1, -1):
                total = total + down * prod_v[8 * k:8 * k + 8, :]
                down = down * d8
            z_v[m:m + 1, :] = jnp.sum(total, axis=0, keepdims=True)

        bias_row = bias_v[...]
        for c in halo_copies:
            c.wait_recv()
        keep = jnp.logical_and(ctx < nctx - 1, lax.broadcasted_iota(jnp.int32, (8, LANES), 0) < 2)
        sig_h = halo[3] * halo[0]
        prod_h = halo[1] * halo[2]
        gs_v[0, TOK:TOK + 8, :] = jnp.where(keep, halo[3] * (halo[4] + bias_row * prod_h), 0.0)
        gs_v[0, 0:TOK, :] = og_v[...] * (sc_v[...] + bias_row * prod_v[...])

        own_cols = pl.ds(pl.multiple_of(z * LANES, LANES), LANES)

        def finish_stream(p):
            taps = sf_v[p]
            g = taps[0:1, :] * gs_v[p, 0:TOK, :]
            g = g + taps[1:2, :] * gs_v[p, 1:TOK + 1, :]
            g = g + taps[2:3, :] * gs_v[p, 2:TOK + 2, :]
            gi_out[p] = g
            abuf[p, :, own_cols] = g.astype(BF16)

        def slot_cols(d):
            return pl.ds(pl.multiple_of(lax.rem(z + d + nz, nz) * LANES, LANES), LANES)

        def a_copy(way, step, p):
            heading = sign if way == 0 else -sign
            ref = abuf.at[p, :, slot_cols(-heading * step)]
            return remote(ref, ref, a_ssem.at[way, step, p], a_rsem.at[way, step, p], at_z(heading))

        def start_own(p):
            a_copy(0, 0, p).start()
            if half > 1:
                a_copy(1, 0, p).start()

        finish_stream(0)
        start_own(0)

        d128 = jnp.exp(-rate_v[...] * float(TOK))

        def join(i, state):
            s = nctx - 1 - i
            f_copy(s, ctx).wait_recv()
            return frecv[s] + d128 * state

        state_in = lax.fori_loop(0, nctx - 1 - ctx, join, zero)

        q = res * state_in
        far = [jnp.zeros((8, LANES), F32) for _ in range(blocks)]
        for m in range(MODES):
            cur = q[m:m + 1, :] * base_v[m]
            d8 = d8_v[m]
            for k in range(blocks - 1, -1, -1):
                far[k] = far[k] + cur
                if k:
                    cur = cur * d8
        corr = corr_v[...] + jnp.concatenate(far, axis=0)
        corr_h0 = jnp.sum(q, axis=0, keepdims=True)
        state_h1 = (state_in - sig_h[0:1, :]) * jnp.exp(rate_v[...])
        corr_h1 = jnp.sum(res * state_h1, axis=0, keepdims=True)
        first_row = lax.broadcasted_iota(jnp.int32, (8, LANES), 0) == 0
        gp_h = jnp.where(first_row, corr_h0, corr_h1) + bias_row * sig_h
        gp = corr + bias_row * sig_v[...]
        gs_v[1, TOK:TOK + 8, :] = jnp.where(keep, gp_h * halo[2], 0.0)
        gs_v[1, 0:TOK, :] = gp * feat_v[2]
        finish_stream(1)
        start_own(1)
        gs_v[2, TOK:TOK + 8, :] = jnp.where(keep, gp_h * halo[1], 0.0)
        gs_v[2, 0:TOK, :] = gp * feat_v[1]
        finish_stream(2)
        start_own(2)

        gsend[0:MODES, :] = near_grad + state_in * z_v[...]
        gsend[MODES:MODES + 8, :] = jnp.broadcast_to(
            jnp.sum(sig_v[...] * prod_v[...], axis=0, keepdims=True), (8, LANES))

        def g_copy(src_ctx, dst):
            return remote(gsend, grecv.at[src_ctx], g_ssem.at[dst], g_rsem.at[src_ctx], at_ctx(dst))

        def send_g(d, carry):
            g_copy(ctx, lax.rem(ctx + d, nctx)).start()
            return carry

        lax.fori_loop(1, nctx, send_g, 0)

        def ring(lo, hi):
            def step_body(step, carry):
                for p in range(3):
                    a_copy(0, step, p).wait_recv()

                    @pl.when(step < half - 1)
                    def _():
                        a_copy(0, step + 1, p).start()

                    @pl.when(step < half - 1)
                    def _():
                        a_copy(1, step, p).wait_recv()

                    @pl.when(step < half - 2)
                    def _():
                        a_copy(1, step + 1, p).start()
                return carry

            lax.fori_loop(lo, hi, step_body, 0)

        marks = [min(half, m) for m in (2, 4, 7, 8)]
        ring(0, marks[0])
        b_out0.wait_recv()
        b_relay0.start()
        b_out1.wait_recv()
        b_relay1.start()
        ring(marks[0], marks[1])

        b_in = [b_right, b_left, b_relay0, b_relay1]
        core_out = [same_place(-1, r0, share_rows, 6, other), same_place(1, r0, share_rows, 7, other),
                    same_place(2, r0, half_rows, 8, other), same_place(2, r0 + half_rows, half_rows, 9, other)]
        y_out = [[same_place(-1, r0, half_rows, 10, at_y(1)), same_place(-1, r0 + half_rows, half_rows, 11, at_y(-1))],
                 [same_place(1, r0, half_rows, 12, at_y(1)), same_place(1, r0 + half_rows, half_rows, 13, at_y(-1))],
                 [same_place(2, r0, half_rows, 14, at_y(1))],
                 [same_place(2, r0 + half_rows, half_rows, 15, at_y(-1))]]
        ry = (2 * (1 - lax.rem(y, 2)) + core) * share_rows
        yc_out = []
        for j, dx in enumerate((-1, 1, 2)):
            yc_out.append(same_place(dx, ry, half_rows, 16 + 2 * j, other))
            yc_out.append(same_place(dx, ry + half_rows, half_rows, 17 + 2 * j, other))
        y_in = [y_out[0][0], y_out[0][1], y_out[1][0], y_out[1][1], y_out[2][0], y_out[3][0]]

        def pass_on(i):
            b_in[i].wait_recv()
            for c in y_out[i]:
                c.start()
            core_out[i].start()

        pass_on(0)
        pass_on(1)
        ring(marks[1], marks[2])
        for i in range(4):
            y_in[i].wait_recv()
            yc_out[i].start()
        pass_on(2)
        pass_on(3)
        ring(marks[2], marks[3])
        for i in range(4, 6):
            y_in[i].wait_recv()
            yc_out[i].start()
        for c in core_out + yc_out:
            c.wait_recv()
        own_w.wait()

        dims = (((1,), (1,)), ((), ()))
        acc = lax.dot_general(abuf[0], wbuf[0], dims, preferred_element_type=F32)
        acc = acc + lax.dot_general(abuf[1], wbuf[1], dims, preferred_element_type=F32)
        acc_v[...] = acc + lax.dot_general(abuf[2], wbuf[2], dims, preferred_element_type=F32)

        def piece(dx):
            return acc_v[:, pl.ds(pl.multiple_of(lax.rem(x + dx, NX) * LANES, LANES), LANES)]

        c_copies = []
        for dx in (2, 1, 3):
            csend[dx - 1] = piece(dx).astype(BF16)
            c = remote(csend.at[dx - 1], crecv.at[dx - 1], c_ssem.at[dx - 1], c_rsem.at[dx - 1], at_x(dx))
            c.start()
            c_copies.append(c)

        def g_wait(d, total):
            s = lax.rem(ctx + d, nctx)
            g_copy(s, ctx).wait_recv()
            return total + grecv[s]

        total = lax.fori_loop(1, nctx, g_wait, gsend[...])
        gr_out[...] = total[0:MODES, :] * scale
        gb_out[...] = total[MODES:MODES + 1, :] * scale

        for c in c_copies:
            c.wait_recv()
        gx_out[...] = ((piece(0) + crecv[0].astype(F32)) + crecv[1].astype(F32)) + crecv[2].astype(F32)

        for c in halo_copies + [b_out0, b_out1, b_right, b_left, b_relay0, b_relay1] + core_out + yc_out + y_in + c_copies:
            c.wait_send()

        def f_sent(i, carry):
            f_copy(ctx, i).wait_send()
            return carry

        lax.fori_loop(0, ctx, f_sent, 0)

        def g_sent(d, carry):
            g_copy(ctx, lax.rem(ctx + d, nctx)).wait_send()
            return carry

        lax.fori_loop(1, nctx, g_sent, 0)

        def a_sent(step, carry):
            for p in range(3):
                a_copy(0, step, p).wait_send()

                @pl.when(step < half - 1)
                def _():
                    a_copy(1, step, p).wait_send()
            return carry

        lax.fori_loop(0, half, a_sent, 0)

    return kernel


def build(nctx, nchan):
    nz = nchan // NX
    half = nz // 2
    width = nz * LANES
    half_rows = LANES // SHARES // 2
    any_spec = pl.BlockSpec(memory_space=pl.ANY)
    vmem_spec = pl.BlockSpec(memory_space=pltpu.VMEM)
    dma = pltpu.SemaphoreType.DMA
    vm = pltpu.VMEM
    call = pl.pallas_call(
        make_kernel(nctx, nz),
        out_shape=(
            jax.ShapeDtypeStruct((3, TOK, LANES), F32),
            jax.ShapeDtypeStruct((TOK, LANES), F32),
            jax.ShapeDtypeStruct((MODES, LANES), F32),
            jax.ShapeDtypeStruct((1, LANES), F32)),
        in_specs=[any_spec] * 8,
        out_specs=(vmem_spec,) * 4,
        scratch_shapes=[
            vm((3, TOK, LANES), F32), vm((TOK, LANES), F32), vm((TOK, LANES), F32),
            vm((3, 3, LANES), F32), vm((MODES, LANES), F32), vm((MODES, LANES), F32), vm((1, LANES), F32),
            vm((TOK, LANES), F32), vm((TOK, LANES), F32), vm((TOK, LANES), F32), vm((3, TOK + 8, LANES), F32),
            vm((MODES, 8, LANES), F32), vm((MODES, 8, LANES), F32), vm((MODES, LANES), F32),
            vm((MODES, LANES), F32), vm((nctx, MODES, LANES), F32), vm((5, 8, LANES), F32),
            vm((MODES + 8, LANES), F32), vm((nctx, MODES + 8, LANES), F32),
            vm((3, TOK, width), BF16), vm((3, NX * LANES, width), BF16), vm((2, 3, half_rows, width), BF16),
            vm((TOK, NX * LANES), F32), vm((NX - 1, TOK, LANES), BF16), vm((NX - 1, TOK, LANES), BF16),
            dma((7,)), dma((1,)), dma((nctx,)), dma((nctx,)), dma((3,)), dma((3,)), dma((nctx,)), dma((nctx,)),
            dma((2, half, 3)), dma((2, half, 3)), dma((22,)), dma((22,)), dma((3,)), dma((3,))],
        compiler_params=pltpu.CompilerParams(
            collective_id=0, has_side_effects=True, vmem_limit_bytes=40 * 1024 * 1024),
    )

    def body(features, saved_conv, out_grad, short_filter, residue, rate, bias, w_proj):
        gi, gx, gr, gb = call(
            features, saved_conv, out_grad, short_filter, residue.T, rate.T, bias.reshape(1, LANES), w_proj)
        return gi, gx, gr.T, gb.reshape(LANES)

    return body


def solution(mesh):
    return jax.shard_map(
        build(mesh.shape["ctx"], mesh.shape["chan"]),
        mesh=mesh,
        in_specs=(
            P(None, "ctx", "chan"),
            P("ctx", "chan"),
            P("ctx", "chan"),
            P(None, None, "chan"),
            P("chan", None),
            P("chan", None),
            P("chan"),
            P(None, "chan", None),
        ),
        out_specs=(P(None, "ctx", "chan"), P("ctx", "chan"), P("chan", None), P("chan")),
        check_vma=False,
    )
```

time: 266 us -> 77.3 us (0.29)
  the two profiles are of different devices: /device:TPU:16 before, /device:TPU:1 now
where the time goes in v1:
time: 77.3 us; the launch traced here: 76.9 us
  Pallas kernels  65.7 us (85%)
  local copies, waits for them, and re-layouts  10.5 us (14%)
    pallas_call x1, Pallas kernels, body(): call(features, saved_conv, out_grad, short_filter, residue.T, rate.T, bia...  65.7 us
    unnamed x20, local copies, waits for them, and re-layouts  10.5 us

profile of v1, /device:TPU:1, one launch (start us, length us, event | category | flops | bytes accessed | tf_op | source)
XLA Modules:
  0.0 76.9 jit_solution(8620026808759268000)
XLA Ops:
  0.6 0.0 copy-start
  0.6 2.8 %copy-done = bf16[3,128,8192]{2,1,0:T(8,128)(2,1)S(1)} copy-done((bf16[3,128,8192]{2,1,0:T(8,128)(2,1)S(1)}, bf16[3,128,8192]{2,1,0:T(8,128)(2,1)}, u32[]{:S(2)}) %copy-start) | copy-done | bytes 6291480
  3.4 0.0 copy-start.1
  3.4 0.9 %copy-done.1 = f32[3,128,128]{2,1,0:T(8,128)S(1)} copy-done((f32[3,128,128]{2,1,0:T(8,128)S(1)}, f32[3,128,128]{2,1,0:T(8,128)}, u32[]{:S(2)}) %copy-start.1) | copy-done | bytes 196632
  4.3 0.0 copy-start.2
  4.3 0.8 %copy-done.2 = f32[128,128]{1,0:T(8,128)S(1)} copy-done((f32[128,128]{1,0:T(8,128)S(1)}, f32[128,128]{1,0:T(8,128)}, u32[]{:S(2)}) %copy-start.2) | copy-done | bytes 65560
  5.2 0.0 copy-start.3
  5.2 0.8 %copy-done.3 = f32[128,128]{1,0:T(8,128)S(1)} copy-done((f32[128,128]{1,0:T(8,128)S(1)}, f32[128,128]{1,0:T(8,128)}, u32[]{:S(2)}) %copy-start.3) | copy-done | bytes 65560
  6.0 0.0 copy-start.4
  6.0 0.7 copy-done.4
  6.7 0.0 copy-start.5
  6.7 0.7 copy-done.5
  7.4 0.0 copy-start.6
  7.4 0.7 copy-done.6
  8.1 0.0 copy-start.7
  8.1 0.7 copy-done.7
  8.8 65.7 %shard_map.111 = (f32[3,128,128]{2,1,0:T(8,128)S(1)}, f32[128,128]{1,0:T(8,128)S(1)}, f32[16,128]{1,0:T(8,128)S(1)}, f32[1,128]{1,0:T(1,128)S(1)}) custom-call(f32[3,128,128]{2,1,0:T(8,128)S(1)} %copy-done.1, f32[128,128]{1,0:T(8,128)S(1)} %copy-done.2, f32[128,128]{1,0:T(8,128)S(1)} %copy-done.3, f32[3,3,128]{2,1,0:T(4,128)S(1)} %copy-done.6, ...), custom_call_target="tpu_custom_call" | custom-call | tf_op jit(solution)/shard_map/pallas_call | solution.py:415
  74.5 0.7 copy.16
  75.2 0.6 copy.17
  75.8 0.6 copy.18
  76.4 0.5 copy.19
Async XLA Ops:
  0.6 2.8 %copy-start = (bf16[3,128,8192]{2,1,0:T(8,128)(2,1)S(1)}, bf16[3,128,8192]{2,1,0:T(8,128)(2,1)}, u32[]{:S(2)}) copy-start(bf16[3,128,8192]{2,1,0:T(8,128)(2,1)} %w.1) | copy-start | bytes 18874372
  3.4 0.9 %copy-start.1 = (f32[3,128,128]{2,1,0:T(8,128)S(1)}, f32[3,128,128]{2,1,0:T(8,128)}, u32[]{:S(2)}) copy-start(f32[3,128,128]{2,1,0:T(8,128)} %feat.1) | copy-start | bytes 589828
  4.3 0.8 %copy-start.2 = (f32[128,128]{1,0:T(8,128)S(1)}, f32[128,128]{1,0:T(8,128)}, u32[]{:S(2)}) copy-start(f32[128,128]{1,0:T(8,128)} %sconv.1) | copy-start | bytes 196612
  5.2 0.8 %copy-start.3 = (f32[128,128]{1,0:T(8,128)S(1)}, f32[128,128]{1,0:T(8,128)}, u32[]{:S(2)}) copy-start(f32[128,128]{1,0:T(8,128)} %ograd.1) | copy-start | bytes 196612
  6.0 0.7 copy-start.4
  6.7 0.7 copy-start.5
  7.4 0.7 copy-start.6
  8.1 0.7 copy-start.7

commit v2 on v1

v2 whole, which is shorter than its diff:
```python
import jax
import jax.numpy as jnp
from jax import lax
from jax.experimental import pallas as pl
from jax.experimental.pallas import tpu as pltpu
from jax.sharding import PartitionSpec as P

NX = 4
MODES = 16
TOK = 128
LANES = 128
SHARES = 4
PARTS = ((0, 0, 16), (1, 0, 16), (2, 0, 8), (2, 8, 4), (2, 12, 4))
X_START, HOP, A_START = 7.7, 3.0, (9.0, 13.0, 13.3)
JUMP = (4, 4, 4)
EARLY = 1
F32 = jnp.float32
BF16 = jnp.bfloat16
MESH = pl.DeviceIdType.MESH


def make_kernel(nctx, nz):
    ny = nctx // 2
    half = nz // 2
    strides = [way * d for d in sorted({1} | {j for j in JUMP if j <= half}) for way in (1, -1)]
    width = nz * LANES
    part = width // 16
    share_rows = LANES // SHARES
    half_rows = share_rows // 2
    scale = (TOK * nctx) ** -0.5
    blocks = TOK // 8

    def kernel(feat, sconv, ograd, sfilt, residue, rate, bias, w,
               gi_out, gx_out, gr_out, gb_out,
               feat_v, sc_v, og_v, sf_v, res_v, rate_v, bias_v, sig_v, prod_v, corr_v, gs_v,
               base_v, d8_v, z_v, fsend, frecv, halo, gsum, grecv, abuf, wbuf,
               acc_v, csend, crecv,
               in_sem, w_sem, f_ssem, f_rsem, h_ssem, h_rsem, g_ssem, g_rsem,
               a_ssem, a_rsem, b_ssem, b_rsem, c_ssem, c_rsem):
        ctx = lax.axis_index("ctx")
        chan = lax.axis_index("chan")
        x = chan // nz
        z = lax.rem(chan, nz)
        y = ctx // 2
        core = lax.rem(ctx, 2)

        def at_x(dx):
            return {"chan": lax.rem(x + dx + NX, NX) * nz + z}

        def at_z(dz):
            return {"chan": x * nz + lax.rem(z + dz + nz, nz)}

        def at_ctx(c):
            return {"ctx": c}

        def at_y(dy):
            return {"ctx": lax.rem(y + dy + ny, ny) * 2 + core}

        other = at_ctx(y * 2 + 1 - core)
        sign = 1 - 2 * core

        def remote(src, dst, ssem, rsem, device):
            return pltpu.make_async_remote_copy(
                src_ref=src, dst_ref=dst, send_sem=ssem, recv_sem=rsem,
                device_id=device, device_id_type=MESH)

        barrier = pltpu.get_barrier_semaphore()

        def greet(d, carry):
            pl.semaphore_signal(barrier, inc=1, device_id=at_ctx(lax.rem(ctx + d, nctx)),
                                device_id_type=MESH)
            return carry

        lax.fori_loop(1, nctx, greet, 0)
        for dx in range(1, NX):
            pl.semaphore_signal(barrier, inc=1, device_id=at_x(dx), device_id_type=MESH)
        for dz in strides:
            pl.semaphore_signal(barrier, inc=1, device_id=at_z(dz), device_id_type=MESH)

        loads = [pltpu.make_async_copy(s, d, in_sem.at[i]) for i, (s, d) in enumerate((
            (feat, feat_v), (ograd, og_v), (rate, rate_v), (residue, res_v), (sconv, sc_v),
            (sfilt, sf_v), (bias, bias_v)))]
        for c in loads:
            c.start()
        own_rows = pl.ds(pl.multiple_of(x * LANES, LANES), LANES)
        own_w = pltpu.make_async_copy(
            w.at[:, :, pl.ds(pl.multiple_of(x * width, LANES), width)],
            wbuf.at[:, own_rows, :], w_sem.at[0])
        own_w.start()
        for c in loads:
            c.wait()

        sig_v[...] = og_v[...] * feat_v[0]
        prod_v[...] = feat_v[1] * feat_v[2]

        iota8 = lax.broadcasted_iota(jnp.int32, (8, LANES), 0).astype(F32)
        for m in range(MODES):
            rm = jnp.broadcast_to(rate_v[m:m + 1, :], (8, LANES))
            d8 = jnp.exp(rm * -8.0)
            up = jnp.exp(-rm * iota8)
            base_v[m] = jnp.exp(-rm * (8.0 - iota8))
            d8_v[m] = d8
            total = jnp.zeros((8, LANES), F32)
            for k in range(blocks):
                total = total + up * sig_v[8 * k:8 * k + 8, :]
                up = up * d8
            fsend[m:m + 1, :] = jnp.sum(total, axis=0, keepdims=True)

        pl.semaphore_wait(barrier, nctx - 1 + NX - 1 + len(strides))

        prev = at_ctx(lax.rem(ctx + nctx - 1, nctx))
        halo_copies = [
            remote(feat.at[:, 0:8, :], halo.at[0:3], h_ssem.at[0], h_rsem.at[0], prev),
            remote(ograd.at[0:8, :], halo.at[3], h_ssem.at[1], h_rsem.at[1], prev),
            remote(sconv.at[0:8, :], halo.at[4], h_ssem.at[2], h_rsem.at[2], prev)]

        def f_copy(src_ctx, dst):
            return remote(fsend, frecv.at[src_ctx], f_ssem.at[dst], f_rsem.at[src_ctx], at_ctx(dst))

        for dy in sorted(range(1, ny), key=lambda d: -min(d, ny - d)):
            @pl.when(y >= dy)
            def _():
                f_copy(ctx, (y - dy) * 2 + core).start()
                f_copy(ctx, (y - dy) * 2 + 1 - core).start()

        @pl.when(core == 1)
        def _():
            f_copy(ctx, y * 2).start()

        for c in halo_copies:
            c.start()

        share = 2 * lax.rem(y, 2) + core
        r0 = share * share_rows

        def rows_of(dx, first, count):
            return pl.ds(pl.multiple_of(lax.rem(x + dx + NX, NX) * LANES + first, 8), count)

        def cols_of(dx, q):
            first = lax.rem(x + dx + NX, NX) * width + PARTS[q][1] * part
            return pl.ds(pl.multiple_of(first, LANES), PARTS[q][2] * part)

        mine = pl.ds(pl.multiple_of(r0, 8), share_rows)
        ry = (2 * (1 - lax.rem(y, 2)) + core) * share_rows
        towards = (2, 1, -1)
        origin = (2, -1, 1)

        def b_fetch(q, j):
            return remote(w.at[PARTS[q][0], mine, cols_of(towards[j], q)],
                          wbuf.at[PARTS[q][0], rows_of(0, r0, share_rows), cols_in(q)],
                          b_ssem.at[0, q, j], b_rsem.at[0, q, j], at_x(towards[j]))

        def cols_in(q):
            return pl.ds(PARTS[q][1] * part, PARTS[q][2] * part)

        def same_place(kind, q, j, first, count, device):
            ref = wbuf.at[PARTS[q][0], rows_of(origin[j], first, count), cols_in(q)]
            return remote(ref, ref, b_ssem.at[kind, q, j], b_rsem.at[kind, q, j], device)

        def b_core(p, j):
            return same_place(1, p, j, r0, share_rows, other)

        def b_up(p, j):
            return same_place(2, p, j, r0, half_rows, at_y(1))

        def b_down(p, j):
            return same_place(3, p, j, r0 + half_rows, half_rows, at_y(-1))

        def b_up_in(p, j):
            return same_place(2, p, j, ry, half_rows, at_y(1))

        def b_down_in(p, j):
            return same_place(3, p, j, ry + half_rows, half_rows, at_y(-1))

        def b_core2(p, j):
            return same_place(4, p, j, ry, share_rows, other)

        pieces = [(q, j) for q in range(len(PARTS)) for j in range(3)]
        for p, j in pieces:
            b_fetch(p, j).start()

        def fetched(p, j):
            b_fetch(p, j).wait_recv()
            b_up(p, j).start()
            b_down(p, j).start()
            b_core(p, j).start()

        def from_y(p, j):
            b_up_in(p, j).wait_recv()
            b_down_in(p, j).wait_recv()
            b_core2(p, j).start()

        dec = jnp.exp(-rate_v[...])
        res = res_v[...]

        def scan_block(i, carry):
            state, total = carry
            first = pl.multiple_of(TOK - 8 - 8 * i, 8)
            sig8 = sig_v[pl.ds(first, 8), :]
            prod8 = prod_v[pl.ds(first, 8), :]
            rows = [None] * 8
            for t in range(7, -1, -1):
                state = sig8[t:t + 1, :] + dec * state
                total = total + prod8[t:t + 1, :] * state
                rows[t] = jnp.sum(res * state, axis=0, keepdims=True)
            corr_v[pl.ds(first, 8), :] = jnp.concatenate(rows, axis=0)
            return state, total

        zero = jnp.zeros((MODES, LANES), F32)
        _, near_grad = lax.fori_loop(0, blocks, scan_block, (zero, zero))

        for m in range(MODES):
            down = base_v[m]
            d8 = d8_v[m]
            total = jnp.zeros((8, LANES), F32)
            for k in range(blocks - 1, -1, -1):
                total = total + down * prod_v[8 * k:8 * k + 8, :]
                down = down * d8
            z_v[m:m + 1, :] = jnp.sum(total, axis=0, keepdims=True)

        bias_row = bias_v[...]
        for c in halo_copies:
            c.wait_recv()
        keep = jnp.logical_and(ctx < nctx - 1, lax.broadcasted_iota(jnp.int32, (8, LANES), 0) < 2)
        sig_h = halo[3] * halo[0]
        prod_h = halo[1] * halo[2]
        gs_v[0, TOK:TOK + 8, :] = jnp.where(keep, halo[3] * (halo[4] + bias_row * prod_h), 0.0)
        gs_v[0, 0:TOK, :] = og_v[...] * (sc_v[...] + bias_row * prod_v[...])

        def finish_stream(p):
            taps = sf_v[p]
            g = taps[0:1, :] * gs_v[p, 0:TOK, :]
            g = g + taps[1:2, :] * gs_v[p, 1:TOK + 1, :]
            g = g + taps[2:3, :] * gs_v[p, 2:TOK + 2, :]
            gi_out[p] = g
            abuf[z, p] = g.astype(BF16)

        reach = (half, half - 1)

        def a_send(way, dist, p):
            heading = sign if way == 0 else -sign
            hops = dist if dist == JUMP[p] else 1
            ref = abuf.at[lax.rem(z - heading * (dist - hops) + nz, nz), p]
            return remote(ref, ref, a_ssem.at[way, dist, p], a_rsem.at[way, dist, p], at_z(heading * hops))

        def a_recv(way, dist, p):
            heading = sign if way == 0 else -sign
            ref = abuf.at[lax.rem(z - heading * dist + nz, nz), p]
            return remote(ref, ref, a_ssem.at[way, dist, p], a_rsem.at[way, dist, p], at_z(heading))

        def start_own(p):
            for dist in sorted({1, JUMP[p]}, reverse=True):
                for way in range(2):
                    if dist <= reach[way]:
                        a_send(way, dist, p).start()

        def passes(way, dist, p):
            return dist + 1 <= reach[way] and dist + 1 != JUMP[p]

        def ring(p, dist):
            for way in range(2):
                if passes(way, dist, p):
                    a_recv(way, dist, p).wait_recv()
                    a_send(way, dist + 1, p).start()

        def ring_ends(p):
            for way in range(2):
                for dist in range(1, reach[way] + 1):
                    if not passes(way, dist, p):
                        a_recv(way, dist, p).wait_recv()

        finish_stream(0)
        start_own(0)

        for dist in range(1, EARLY + 1):
            ring(0, dist)

        d128 = jnp.exp(-rate_v[...] * float(TOK))

        def join(i, state):
            s = nctx - 1 - i
            f_copy(s, ctx).wait_recv()
            return frecv[s] + d128 * state

        state_in = lax.fori_loop(0, nctx - 1 - ctx, join, zero)

        q = res * state_in
        far = [jnp.zeros((8, LANES), F32) for _ in range(blocks)]
        for m in range(MODES):
            cur = q[m:m + 1, :] * base_v[m]
            d8 = d8_v[m]
            for k in range(blocks - 1, -1, -1):
                far[k] = far[k] + cur
                if k:
                    cur = cur * d8
        corr = corr_v[...] + jnp.concatenate(far, axis=0)
        corr_h0 = jnp.sum(q, axis=0, keepdims=True)
        state_h1 = (state_in - sig_h[0:1, :]) * jnp.exp(rate_v[...])
        corr_h1 = jnp.sum(res * state_h1, axis=0, keepdims=True)
        first_row = lax.broadcasted_iota(jnp.int32, (8, LANES), 0) == 0
        gp_h = jnp.where(first_row, corr_h0, corr_h1) + bias_row * sig_h
        gp = corr + bias_row * sig_v[...]
        gs_v[1, TOK:TOK + 8, :] = jnp.where(keep, gp_h * halo[2], 0.0)
        gs_v[1, 0:TOK, :] = gp * feat_v[2]
        finish_stream(1)
        start_own(1)
        gs_v[2, TOK:TOK + 8, :] = jnp.where(keep, gp_h * halo[1], 0.0)
        gs_v[2, 0:TOK, :] = gp * feat_v[1]
        finish_stream(2)
        start_own(2)

        gsum[0, 0:MODES, :] = near_grad + state_in * z_v[...]
        gsum[0, MODES:MODES + 8, :] = jnp.broadcast_to(
            jnp.sum(sig_v[...] * prod_v[...], axis=0, keepdims=True), (8, LANES))

        g_pair = remote(gsum.at[0], grecv.at[ny], g_ssem.at[0], g_rsem.at[0], other)
        g_pair.start()

        def g_copy(src, dy):
            return remote(gsum.at[1], grecv.at[src], g_ssem.at[dy], g_rsem.at[1 + src], at_y(dy))

        def g_chip():
            g_pair.wait_recv()
            chip = gsum[0] + grecv[ny]
            gsum[1] = chip
            grecv[y] = chip
            for dy in range(1, ny):
                g_copy(y, dy).start()

        events = []
        for dist in range(1, half + 1):
            for p in range(3):
                took = HOP * (dist if dist < JUMP[p] else dist - JUMP[p] + 0.7 + 0.3 * JUMP[p])
                if p or dist > EARLY:
                    events.append((A_START[p] + took, lambda p=p, dist=dist: ring(p, dist)))
        before = 0
        for q, (_, _, size) in enumerate(PARTS):
            for j in range(3):
                at = X_START + 18.3 / 48 * (before + size * (0.8, 0.95, 1.0)[j])
                events.append((at, lambda q=q, j=j: fetched(q, j)))
                events.append((at + 3.0 + 13.7 / 48 * size, lambda q=q, j=j: from_y(q, j)))
            before += size
        events.append((A_START[2] + 3.0, g_chip))
        for _, act in sorted(events, key=lambda e: e[0]):
            act()

        own_w.wait()
        dims = (((1,), (1,)), ((), ()))

        def product_of(p):
            for q, j in pieces:
                if PARTS[q][0] == p:
                    b_core(q, j).wait_recv()
                    b_core2(q, j).wait_recv()
            ring_ends(p)
            column = jnp.concatenate([abuf[slot, p] for slot in range(nz)], axis=1)
            return lax.dot_general(column, wbuf[p], dims, preferred_element_type=F32)

        acc_v[...] = product_of(0) + product_of(1)
        acc_v[...] += product_of(2)

        def piece(dx):
            return acc_v[:, pl.ds(pl.multiple_of(lax.rem(x + dx, NX) * LANES, LANES), LANES)]

        c_copies = []
        for dx in (2, 1, 3):
            csend[dx - 1] = piece(dx).astype(BF16)
            c = remote(csend.at[dx - 1], crecv.at[dx - 1], c_ssem.at[dx - 1], c_rsem.at[dx - 1], at_x(dx))
            c.start()
            c_copies.append(c)

        for src in range(1, ny):
            s = lax.rem(y + src, ny)
            g_copy(s, src).wait_recv()
        total = grecv[0]
        for src in range(1, ny):
            total = total + grecv[src]
        gr_out[...] = total[0:MODES, :] * scale
        gb_out[...] = total[MODES:MODES + 1, :] * scale

        for c in c_copies:
            c.wait_recv()
        gx_out[...] = ((piece(0) + crecv[0].astype(F32)) + crecv[1].astype(F32)) + crecv[2].astype(F32)

        for c in halo_copies + c_copies:
            c.wait_send()
        for p, j in pieces:
            for make in (b_fetch, b_core, b_up, b_down, b_core2):
                make(p, j).wait_send()
        g_pair.wait_send()
        for dy in range(1, ny):
            g_copy(y, dy).wait_send()

        def f_sent(i, carry):
            f_copy(ctx, i).wait_send()
            return carry

        lax.fori_loop(0, ctx, f_sent, 0)

        for p in range(3):
            for way in range(2):
                for dist in range(1, reach[way] + 1):
                    a_send(way, dist, p).wait_send()

    return kernel


def build(nctx, nchan):
    nz = nchan // NX
    half = nz // 2
    width = nz * LANES
    ny = nctx // 2
    any_spec = pl.BlockSpec(memory_space=pl.ANY)
    vmem_spec = pl.BlockSpec(memory_space=pltpu.VMEM)
    dma = pltpu.SemaphoreType.DMA
    vm = pltpu.VMEM
    shapes = (
        jax.ShapeDtypeStruct((3, TOK, LANES), F32),
        jax.ShapeDtypeStruct((TOK, LANES), F32),
        jax.ShapeDtypeStruct((MODES, LANES), F32),
        jax.ShapeDtypeStruct((1, LANES), F32))
    call = pl.pallas_call(
        make_kernel(nctx, nz),
        out_shape=shapes,
        in_specs=[any_spec] * 8,
        out_specs=(vmem_spec,) * 4,
        scratch_shapes=[
            vm((3, TOK, LANES), F32), vm((TOK, LANES), F32), vm((TOK, LANES), F32),
            vm((3, 3, LANES), F32), vm((MODES, LANES), F32), vm((MODES, LANES), F32), vm((1, LANES), F32),
            vm((TOK, LANES), F32), vm((TOK, LANES), F32), vm((TOK, LANES), F32), vm((3, TOK + 8, LANES), F32),
            vm((MODES, 8, LANES), F32), vm((MODES, 8, LANES), F32), vm((MODES, LANES), F32),
            vm((MODES, LANES), F32), vm((nctx, MODES, LANES), F32), vm((5, 8, LANES), F32),
            vm((2, MODES + 8, LANES), F32), vm((ny + 1, MODES + 8, LANES), F32),
            vm((nz, 3, TOK, LANES), BF16), vm((3, NX * LANES, width), BF16),
            vm((TOK, NX * LANES), F32), vm((NX - 1, TOK, LANES), BF16), vm((NX - 1, TOK, LANES), BF16),
            dma((7,)), dma((1,)), dma((nctx,)), dma((nctx,)), dma((3,)), dma((3,)), dma((ny,)), dma((ny + 1,)),
            dma((2, nz // 2 + 1, 3)), dma((2, nz // 2 + 1, 3)), dma((5, len(PARTS), 3)), dma((5, len(PARTS), 3)), dma((3,)), dma((3,))],
        compiler_params=pltpu.CompilerParams(
            collective_id=0, has_side_effects=True, vmem_limit_bytes=40 * 1024 * 1024),
    )

    def put_out_kernel(*refs):
        sources, targets, sem = refs[:4], refs[4:8], refs[8]
        copies = [pltpu.make_async_copy(a, b, sem.at[i]) for i, (a, b) in enumerate(zip(sources, targets))]
        for c in copies:
            c.start()
        for c in copies:
            c.wait()

    put_out = pl.pallas_call(
        put_out_kernel,
        out_shape=shapes,
        in_specs=[vmem_spec] * 4,
        out_specs=(any_spec,) * 4,
        scratch_shapes=[dma((4,))],
        compiler_params=pltpu.CompilerParams(vmem_limit_bytes=8 * 1024 * 1024),
    )

    def body(features, saved_conv, out_grad, short_filter, residue, rate, bias, w_proj):
        operands = (features, saved_conv, out_grad, short_filter, residue.T, rate.T, bias.reshape(1, LANES), w_proj)
        gi, gx, gr, gb = put_out(*call(*[pltpu.with_memory_space_constraint(v, pltpu.HBM) for v in operands]))
        return gi, gx, gr.T, gb.reshape(LANES)

    return body


def solution(mesh):
    return jax.shard_map(
        build(mesh.shape["ctx"], mesh.shape["chan"]),
        mesh=mesh,
        in_specs=(
            P(None, "ctx", "chan"),
            P("ctx", "chan"),
            P("ctx", "chan"),
            P(None, None, "chan"),
            P("chan", None),
            P("chan", None),
            P("chan"),
            P(None, "chan", None),
        ),
        out_specs=(P(None, "ctx", "chan"), P("ctx", "chan"), P("chan", None), P("chan")),
        check_vma=False,
    )
```

time: 77.3 us -> 63.2 us (0.82)
  local copies, waits for them, and re-layouts: 10.5 us -> 0 us
  Pallas kernels: 65.7 us -> 62.1 us
    unnamed x20 -> x0, local copies, waits for them, and re-layouts: 10.5 us -> none
    pallas_call x1 -> x2, Pallas kernels: 65.7 us -> 62.1 us  [the longest x1 61.4 us: body(): call(*[pltpu.with_memory_space_constraint(v, pltpu.HBM) for v in operands])]
where the time goes in v2:
time: 63.2 us; the launch traced here: 62.7 us
  Pallas kernels  62.1 us (98%)
  between operations  0.64 us (1%)
    pallas_call x1, Pallas kernels, body(): call(*[pltpu.with_memory_space_constraint(v, pltpu.HBM) for v in operands])  61.4 us

profile of v2, /device:TPU:1, one launch (start us, length us, event | category | flops | bytes accessed | tf_op | source)
XLA Modules:
  0.0 62.7 jit_solution(7866807581645787045)
XLA Ops:
  0.6 61.4 %shard_map.111 = (f32[3,128,128]{2,1,0:T(8,128)S(1)}, f32[128,128]{1,0:T(8,128)S(1)}, f32[16,128]{1,0:T(8,128)S(1)}, f32[1,128]{1,0:T(1,128)S(1)}) custom-call(f32[3,128,128]{2,1,0:T(8,128)} %feat.1, f32[128,128]{1,0:T(8,128)} %sconv.1, f32[128,128]{1,0:T(8,128)} %ograd.1, f32[3,3,128]{2,1,0:T(4,128)} %sfilt.1, f32[16,128]{1,0:T(8,128)} %bitcast.5, ...), custom_call_target="tpu_custom_call" | custom-call | tf_op jit(solution)/shard_map/pallas_call | solution.py:461
  62.0 0.7 %shard_map.112 = (f32[3,128,128]{2,1,0:T(8,128)}, f32[128,128]{1,0:T(8,128)}, f32[16,128]{1,0:T(8,128)}, f32[1,128]{1,0:T(1,128)}) custom-call(f32[3,128,128]{2,1,0:T(8,128)S(1)} %get-tuple-element.12.refs_0_, f32[128,128]{1,0:T(8,128)S(1)} %get-tuple-element.13.refs_1_, f32[16,128]{1,0:T(8,128)S(1)} %get-tuple-element.14.refs_2_, ...), custom_call_target="tpu_custom_call" | custom-call | tf_op jit(solution)/shard_map/pallas_call | solution.py:461

commit v3 on v2

--- a/solution.py
+++ b/solution.py
@@ -11,7 +11,7 @@
 LANES = 128
 SHARES = 4
 PARTS = ((0, 0, 16), (1, 0, 16), (2, 0, 8), (2, 8, 4), (2, 12, 4))
-X_START, HOP, A_START = 7.7, 3.0, (9.0, 13.0, 13.3)
+X_START, HOP, A_START = 7.7, 4.0, (9.0, 13.0, 13.3)
 JUMP = (4, 4, 4)
 EARLY = 1
 F32 = jnp.float32
@@ -117,6 +117,8 @@
         def f_copy(src_ctx, dst):
             return remote(fsend, frecv.at[src_ctx], f_ssem.at[dst], f_rsem.at[src_ctx], at_ctx(dst))
 
+        for c in halo_copies:
+            c.start()
         for dy in sorted(range(1, ny), key=lambda d: -min(d, ny - d)):
             @pl.when(y >= dy)
             def _():
@@ -126,9 +128,6 @@
         @pl.when(core == 1)
         def _():
             f_copy(ctx, y * 2).start()
-
-        for c in halo_copies:
-            c.start()
 
         share = 2 * lax.rem(y, 2) + core
         r0 = share * share_rows
@@ -249,7 +248,7 @@
             return remote(ref, ref, a_ssem.at[way, dist, p], a_rsem.at[way, dist, p], at_z(heading))
 
         def start_own(p):
-            for dist in sorted({1, JUMP[p]}, reverse=True):
+            for dist in sorted({1, JUMP[p]}, reverse=p > 0):
                 for way in range(2):
                     if dist <= reach[way]:
                         a_send(way, dist, p).start()

time: 63.2 us -> 61.8 us (0.978)
  Pallas kernels: 62.1 us -> 60.9 us
    pallas_call x1, Pallas kernels: 61.4 us -> 60.2 us  [body(): call(*[pltpu.with_memory_space_constraint(v, pltpu.HBM) for v in operands])]
where the time goes in v3:
time: 61.8 us; the launch traced here: 61.5 us
  Pallas kernels  60.9 us (99%)
  between operations  0.64 us (1%)
    pallas_call x1, Pallas kernels, body(): call(*[pltpu.with_memory_space_constraint(v, pltpu.HBM) for v in operands])  60.2 us

profile of v3, /device:TPU:1, one launch (start us, length us, event | category | flops | bytes accessed | tf_op | source)
XLA Modules:
  0.0 61.5 jit_solution(17213345695372332002)
XLA Ops:
  0.6 60.2 %shard_map.111 = (f32[3,128,128]{2,1,0:T(8,128)S(1)}, f32[128,128]{1,0:T(8,128)S(1)}, f32[16,128]{1,0:T(8,128)S(1)}, f32[1,128]{1,0:T(1,128)S(1)}) custom-call(f32[3,128,128]{2,1,0:T(8,128)} %feat.1, f32[128,128]{1,0:T(8,128)} %sconv.1, f32[128,128]{1,0:T(8,128)} %ograd.1, f32[3,3,128]{2,1,0:T(4,128)} %sfilt.1, f32[16,128]{1,0:T(8,128)} %bitcast.5, ...), custom_call_target="tpu_custom_call" | custom-call | tf_op jit(solution)/shard_map/pallas_call | solution.py:460
  60.8 0.7 %shard_map.112 = (f32[3,128,128]{2,1,0:T(8,128)}, f32[128,128]{1,0:T(8,128)}, f32[16,128]{1,0:T(8,128)}, f32[1,128]{1,0:T(1,128)}) custom-call(f32[3,128,128]{2,1,0:T(8,128)S(1)} %get-tuple-element.12.refs_0_, f32[128,128]{1,0:T(8,128)S(1)} %get-tuple-element.13.refs_1_, f32[16,128]{1,0:T(8,128)S(1)} %get-tuple-element.14.refs_2_, ...), custom_call_target="tpu_custom_call" | custom-call | tf_op jit(solution)/shard_map/pallas_call | solution.py:460

commit v4 on v3

--- a/solution.py
+++ b/solution.py
@@ -248,7 +248,7 @@
             return remote(ref, ref, a_ssem.at[way, dist, p], a_rsem.at[way, dist, p], at_z(heading))
 
         def start_own(p):
-            for dist in sorted({1, JUMP[p]}, reverse=p > 0):
+            for dist in sorted({1, JUMP[p]}):
                 for way in range(2):
                     if dist <= reach[way]:
                         a_send(way, dist, p).start()

time: 61.8 us -> 61.4 us (level)
  no operation moved by 1% of the time
where the time goes in v4:
time: 61.4 us; the launch traced here: 61.2 us
  Pallas kernels  60.5 us (99%)
  between operations  0.64 us (1%)
    pallas_call x1, Pallas kernels, body(): call(*[pltpu.with_memory_space_constraint(v, pltpu.HBM) for v in operands])  59.8 us

profile of v4, /device:TPU:1, one launch (start us, length us, event | category | flops | bytes accessed | tf_op | source)
XLA Modules:
  0.0 61.2 jit_solution(2110821445755706634)
XLA Ops:
  0.6 59.8 %shard_map.111 = (f32[3,128,128]{2,1,0:T(8,128)S(1)}, f32[128,128]{1,0:T(8,128)S(1)}, f32[16,128]{1,0:T(8,128)S(1)}, f32[1,128]{1,0:T(1,128)S(1)}) custom-call(f32[3,128,128]{2,1,0:T(8,128)} %feat.1, f32[128,128]{1,0:T(8,128)} %sconv.1, f32[128,128]{1,0:T(8,128)} %ograd.1, f32[3,3,128]{2,1,0:T(4,128)} %sfilt.1, f32[16,128]{1,0:T(8,128)} %bitcast.5, ...), custom_call_target="tpu_custom_call" | custom-call | tf_op jit(solution)/shard_map/pallas_call | solution.py:460
  60.4 0.7 %shard_map.112 = (f32[3,128,128]{2,1,0:T(8,128)}, f32[128,128]{1,0:T(8,128)}, f32[16,128]{1,0:T(8,128)}, f32[1,128]{1,0:T(1,128)}) custom-call(f32[3,128,128]{2,1,0:T(8,128)S(1)} %get-tuple-element.12.refs_0_, f32[128,128]{1,0:T(8,128)S(1)} %get-tuple-element.13.refs_1_, f32[16,128]{1,0:T(8,128)S(1)} %get-tuple-element.14.refs_2_, ...), custom_call_target="tpu_custom_call" | custom-call | tf_op jit(solution)/shard_map/pallas_call | solution.py:460
